TPU v7x, 32 devices: a whole 2x2x4 slice. The times are simulated.
32 devices in a mesh: row: 2 (over core), col: 4 (over y, x), ch: 4 (over z).
Axes of the slice: x: 2, y: 2, z: 4, core: 2. Of those that a mesh axis runs over, the one named last changes fastest.
Arguments:
- grad_out: float32 [4096, 1024], P(('row', 'col'), 'ch'), may hold values from -6 to 6
- relu_mask: int32 [4096, 1024], P(('row', 'col'), 'ch'), may hold values 0 or 1
- saved_agg: float32 [4096, 1024], P(('row', 'col'), 'ch'), may hold values from -0.1875 to 0.1875
- weight: float32 [1024, 1024], P('ch'), may hold values from -0.1875 to 0.1875
- tile_vals: float32 [2, 4, 128, 128, 128], P('row', 'col'), may hold values from -0.125 to 0.125
- tile_pos: int32 [2, 4, 128], P('row', 'col'), may hold values from 0 to 127, as said below
- tile_count: int32 [2, 4], P('row', 'col'), may hold values from 32 to 128, as said below
Outputs:
- weight_grad: float32 [1024, 1024], P(('row', 'col'), 'ch')
- input_grad: float32 [4096, 1024], P('col', 'ch')
Inputs may be any that keep to these rules, and one draw needn't show every extreme that they name: `tile_pos`: each block's entries are a permutation of 0 to 127; the first tile_count of them are the block's nonzero tiles, the others list its zero tiles and their slots' values are ignored. `tile_count`: some block is full in every draw.
All inputs are finite; a program needn't handle non-finite values. No bound on the sum of `relu_mask` on one device may be relied on, other than what follows from the above.
Results may differ from a plain program's by a relative error of at most 0.0003.
Values sent between devices are 32-bit elements; how exact they have to be, the bound alone decides.
A program may use at most 128 MiB of HBM per device.

v0:
```python
import jax
import jax.numpy as jnp
from jax import lax
from jax.sharding import PartitionSpec as P

TILE = 128
OUT_TILES = 16
IN_TILES = 8
HIGHEST = lax.Precision.HIGHEST


def block_grad(tile_set, positions, live_count, grad_rows):
    slot_total = tile_set.shape[0]
    channels = grad_rows.shape[1]
    active = (jnp.arange(slot_total, dtype=jnp.int32) < live_count).astype(jnp.float32)
    out_tile = positions // IN_TILES
    in_tile = positions % IN_TILES
    blocks = grad_rows.reshape(OUT_TILES, TILE, channels)
    picked = jnp.take(blocks, out_tile, axis=0)
    product = jnp.einsum("tij,tif->tjf", tile_set, picked, precision=HIGHEST)
    onehot = (in_tile[:, None] == jnp.arange(IN_TILES, dtype=jnp.int32)[None, :]).astype(
        jnp.float32
    ) * active[:, None]
    summed = jnp.einsum("tc,tjf->cjf", onehot, product, precision=HIGHEST)
    return summed.reshape(IN_TILES * TILE, channels)


def per_device(grad_out, relu_mask, saved_agg, weight, tile_vals, tile_pos, tile_count):
    masked = grad_out * relu_mask.astype(jnp.float32)
    contract_rows = (((0,), (0,)), ((), ()))
    full_masked = lax.all_gather(masked, "ch", axis=1, tiled=True)
    partial_value = lax.dot_general(
        saved_agg, full_masked, contract_rows, precision=HIGHEST, preferred_element_type=jnp.float32
    )
    regrouped = lax.all_to_all(partial_value, "ch", split_axis=1, concat_axis=0, tiled=True)
    weight_grad = lax.psum_scatter(regrouped, ("row", "col"), scatter_dimension=0, tiled=True)
    agg_grad = lax.dot_general(
        full_masked,
        weight,
        (((1,), (1,)), ((), ())),
        precision=HIGHEST,
        preferred_element_type=jnp.float32,
    )
    grad_rows = lax.all_gather(agg_grad, "col", axis=0, tiled=True)
    partial_input = block_grad(tile_vals[0, 0], tile_pos[0, 0], tile_count[0, 0], grad_rows)
    input_grad = lax.psum(partial_input, "row")
    return (weight_grad, input_grad)


def solution(mesh):
    in_specs = (
        P(("row", "col"), "ch"),
        P(("row", "col"), "ch"),
        P(("row", "col"), "ch"),
        P("ch", None),
        P("row", "col", None, None, None),
        P("row", "col", None),
        P("row", "col"),
    )
    out_specs = (P(("row", "col"), "ch"), P("col", "ch"))
    return jax.shard_map(
        per_device, mesh=mesh, in_specs=in_specs, out_specs=out_specs, check_vma=False
    )
```

profile of v0, /device:TPU:0, one launch (start us, length us, event | category | flops | bytes accessed | tf_op | source)
XLA Modules:
  0.0 203.6 jit_solution(18225518108952591362)
XLA Ops:
  7.2 0.0 all-gather.3.cloned.1.call-start
  7.2 2.1 %convert_multiply_fusion = f32[512,256]{1,0:T(8,128)} fusion(f32[512,256]{1,0:T(8,128)} %param.7, s32[512,256]{1,0:T(8,128)} %param.8), kind=kLoop, calls=%fused_computation.8 | loop fusion | flops 262144 | bytes 1572864 | tf_op jit(solution)/shard_map/mul | solution.py:29
  9.4 0.0 all-gather.3.cloned.1.call-update
  9.4 0.0 all-gather.5.cloned.1.call-start
  9.4 49.1 %all-gather.3.cloned.1.call-done = f32[512,1024]{1,0:T(8,128)} async-done(((f32[512,256]{1,0:T(8,128)}), f32[512,1024]{1,0:T(8,128)}) %all-gather.3.cloned.1.call-update) | async-done | bytes 2097168 | tf_op jit(solution)/shard_map/all_gather | solution.py:31
  58.5 4.2 %fusion.16 = f32[512,256]{1,0:T(8,128)} fusion(f32[512,1024]{1,0:T(8,128)} %all-gather.3.cloned.1.call-done, f32[256,1024]{1,0:T(8,128)S(1)} %copy-done), kind=kOutput, calls=%fused_computation.35 | convolution fusion | flops 1610612736 | bytes 3670016 | tf_op jit(solution)/shard_map/dot_general | solution.py:37
  62.8 6.1 %fusion.15 = f32[1024,256]{1,0:T(8,128)} fusion(f32[512,1024]{1,0:T(8,128)} %all-gather.3.cloned.1.call-done, f32[512,256]{1,0:T(8,128)} %param.9), kind=kOutput, calls=%fused_computation.34 | convolution fusion | flops 1610612736 | bytes 3670016 | tf_op jit(solution)/shard_map/dot_general | solution.py:32
  68.9 3.5 %all-to-all-start = ((f32[256,4,256]{0,2,1:T(8,128)}), f32[256,4,256]{0,2,1:T(8,128)S(1)}, u32[]{:S(2)}, u32[]{:S(2)}) async-start(f32[256,4,256]{0,2,1:T(8,128)} %bitcast.1), calls=%async_computation | async-start | bytes 2097152 | tf_op jit(solution)/shard_map/all_to_all | solution.py:35
  72.4 0.0 reduce-scatter.2.cloned.1.call-start
  73.1 0.7 fusion.12
  73.8 0.7 compare_and_fusion
  74.5 0.7 and_select_fusion.2
  75.1 23.1 %all-to-all-done = f32[256,4,256]{0,2,1:T(8,128)S(1)} async-done(((f32[256,4,256]{0,2,1:T(8,128)}), f32[256,4,256]{0,2,1:T(8,128)S(1)}, u32[]{:S(2)}, u32[]{:S(2)}) %all-to-all-start) | async-done | bytes 1048608 | tf_op jit(solution)/shard_map/all_to_all | solution.py:35
  98.2 1.3 copy.10
  99.5 0.2 all-reduce.2.cloned.1.call-start
  99.8 0.0 all-gather.5.cloned.1.call-done
  99.8 11.7 %gather_fusion = f32[128,128,256]{2,1,0:T(8,128)} fusion(f32[16,128,256]{2,1,0:T(8,128)} %bitcast.51, s32[1024]{0:T(1024)S(1)} %pad_clamp_fusion), kind=kCustom, calls=%fused_computation | custom fusion | bytes 33554944 | tf_op jit(solution)/shard_map/jit(_take)/gather | solution.py:19
  111.5 34.6 %fusion.2 = f32[128,256,128]{2,1,0:T(8,128)} fusion(f32[128,128,256]{2,1,0:T(8,128)} %gather_fusion, f32[1,1,128,128,128]{4,3,2,1,0:T(8,128)} %param.11, pred[128]{0:T(512)(128)(4,1)S(1)} %compare_and_fusion), kind=kOutput, calls=%fused_computation.3 | convolution fusion | flops 6446645248 | bytes 41943168 | tf_op jit(solution)/shard_map/tij,tif->tjf/dot_general | solution.py:20
  146.1 17.8 %copy.12 = f32[128,256,128]{1,0,2:T(8,128)} copy(f32[128,256,128]{2,1,0:T(8,128)} %fusion.2) | data formatting | bytes 33554432 | tf_op jit(solution)/shard_map/tij,tif->tjf/dot_general | solution.py:20
  163.8 10.8 %fusion = f32[8,128,256]{2,0,1:T(8,128)S(1)} fusion(f32[128,256,128]{1,0,2:T(8,128)} %copy.12, f32[128]{0:T(128)S(1)} %compare_convert_fusion, s32[128]{0:T(128)S(1)} %and_select_fusion.2), kind=kOutput, calls=%fused_computation.1 | convolution fusion | flops 402655232 | bytes 17826816 | tf_op jit(solution)/shard_map/tc,tjf->cjf/dot_general | solution.py:24
  174.7 1.3 copy.11
  176.0 0.0 reduce-scatter.2.cloned.1.call-done
  176.1 18.7 %all-reduce.2.cloned.1.call-done = f32[1024,256]{1,0:T(8,128)} async-done(((f32[1024,256]{1,0:T(8,128)}), f32[1024,256]{1,0:T(8,128)}) %all-reduce.2.cloned.1.call-update) | async-done | bytes 1048592 | tf_op jit(solution)/shard_map/psum | solution.py:46
  194.8 2.3 %copy.15 = f32[1024,256]{1,0:T(8,128)} copy(f32[1024,256]{1,0:T(8,128)} %all-reduce.2.cloned.1.call-done) | data formatting | bytes 2097152
  (9 shorter events, 0.1 us)
Async XLA Ops:
  7.2 51.4 %copy-start = (f32[256,1024]{1,0:T(8,128)S(1)}, f32[256,1024]{1,0:T(8,128)}, u32[]{:S(2)}) copy-start(f32[256,1024]{1,0:T(8,128)} %param.10) | copy-start | bytes 3145732
  7.2 51.4 %all-gather.3.cloned.1.call-start = ((), (), s32[]{:S(2)}) async-start(), calls=%async_computation.2 | async-start | bytes 2621440 | tf_op jit(solution)/shard_map/all_gather | solution.py:31
  9.4 90.4 %all-gather.5.cloned.1.call-start = ((), (), s32[]{:S(2)}) async-start(), calls=%async_computation.4 | async-start | bytes 2621440 | tf_op jit(solution)/shard_map/all_gather | solution.py:44
  68.9 29.3 %all-to-all-start = ((f32[256,4,256]{0,2,1:T(8,128)}), f32[256,4,256]{0,2,1:T(8,128)S(1)}, u32[]{:S(2)}, u32[]{:S(2)}) async-start(f32[256,4,256]{0,2,1:T(8,128)} %bitcast.1), calls=%async_computation | async-start | bytes 2097152 | tf_op jit(solution)/shard_map/all_to_all | solution.py:35
  72.4 103.7 %reduce-scatter.2.cloned.1.call-start = ((), (), s32[]{:S(2)}) async-start(), calls=%async_computation.3 | async-start | bytes 1179648 | tf_op jit(solution)/shard_map/reduce_scatter | solution.py:36
  99.5 95.2 %all-reduce.2.cloned.1.call-start = ((), (), s32[]{:S(2)}) async-start(), calls=%async_computation.5 | async-start | bytes 2097152 | tf_op jit(solution)/shard_map/psum | solution.py:46
  146.1 51.0 %copy-start.1 = (f32[256,1024]{1,0:T(8,128)S(1)}, f32[256,1024]{1,0:T(8,128)}, u32[]{:S(2)}) copy-start(f32[256,1024]{1,0:T(8,128)} %param.10) | copy-start | bytes 3145732
Sparse Core Ops, SparseCore 0:
  10.1 48.3 all-gather.2
  62.9 33.9 all-gather.4
  100.7 35.9 reduce-scatter.1
  176.2 18.5 all-reduce.1
where the time goes:
time: 204 us
  waiting for transfers between devices  91 us (45%)
  matrix products  55.7 us (27%)
  local copies, waits for them, and re-layouts  34.4 us (17%)
  between operations  14.5 us (7%)
  other arithmetic  4.15 us (2%)
  starting transfers between devices  3.86 us (2%)
    all_gather x1, waiting for transfers between devices, per_device(): full_masked = lax.all_gather(masked, 'ch', axis=1, tiled=True)  49.1 us
    dot_general x1, matrix products, block_grad(): product = jnp.einsum('tij,tif->tjf', tile_set, picked, precision=HIGHEST)  34.6 us
    all_to_all x1, waiting for transfers between devices, per_device(): lax.all_to_all(partial_value, 'ch', split_axis=1, concat_axis=0, tiled=True)  23.1 us
    psum x1, waiting for transfers between devices, per_device(): input_grad = lax.psum(partial_input, 'row')  18.7 us
    dot_general x1, local copies, waits for them, and re-layouts, block_grad(): product = jnp.einsum('tij,tif->tjf', tile_set, picked, precision=HIGHEST)  17.8 us
    gather x1, local copies, waits for them, and re-layouts, block_grad(): picked = jnp.take(blocks, out_tile, axis=0)  11.7 us
    dot_general x1, matrix products, block_grad(): summed = jnp.einsum('tc,tjf->cjf', onehot, product, precision=HIGHEST)  10.8 us
    dot_general x1, matrix products, per_device(): lax.dot_general(saved_agg, full_masked, contract_rows, precision=HIGHEST,...  6.08 us
  transfers between devices with their start and end apart: 5, of which 3 were waited for; matrix products, arithmetic and copies ran while one was open for 42% of the time, Pallas kernels for 0%

commit v1 on v0

--- a/solution.py
+++ b/solution.py
@@ -7,6 +7,7 @@
 OUT_TILES = 16
 IN_TILES = 8
 HIGHEST = lax.Precision.HIGHEST
+wait_digits = lambda block_here: jnp.sum(lax.all_gather(block_here, axis_name="row"), axis=0)
 
 
 def block_grad(tile_set, positions, live_count, grad_rows):
@@ -43,7 +44,7 @@
     )
     grad_rows = lax.all_gather(agg_grad, "col", axis=0, tiled=True)
     partial_input = block_grad(tile_vals[0, 0], tile_pos[0, 0], tile_count[0, 0], grad_rows)
-    input_grad = lax.psum(partial_input, "row")
+    input_grad = wait_digits(partial_input)
     return (weight_grad, input_grad)
 
 

time: 204 us -> 250 us (1.23)
  blocking collectives: 0 us -> 29.9 us
  waiting for transfers between devices: 91 us -> 112 us
  starting transfers between devices: 3.86 us -> 0.34 us
  other arithmetic: 4.15 us -> 6.97 us
  local copies, waits for them, and re-layouts: 34.4 us -> 31.9 us
    reduce_scatter x1, waiting for transfers between devices: 0.02 us -> 31.4 us  [per_device(): lax.psum_scatter(regrouped, ('row', 'col'), scatter_dimension=0, tiled=True)]
    all_gather x1, waiting for transfers between devices: 0.02 us -> 31.2 us  [per_device(): grad_rows = lax.all_gather(agg_grad, 'col', axis=0, tiled=True)]
    all_to_all x0 -> x1, blocking collectives: none -> 29.9 us  [per_device(): lax.all_to_all(partial_value, 'ch', split_axis=1, concat_axis=0, tiled=True)]
    all_to_all x1 -> x0, waiting for transfers between devices: 23.1 us -> none  [per_device(): lax.all_to_all(partial_value, 'ch', split_axis=1, concat_axis=0, tiled=True)]
    psum x1 -> x0, waiting for transfers between devices: 18.7 us -> none  [per_device(): input_grad = lax.psum(partial_input, 'row')]
    all_to_all x1 -> x0, starting transfers between devices: 3.52 us -> none  [per_device(): lax.all_to_all(partial_value, 'ch', split_axis=1, concat_axis=0, tiled=True)]
    reduce_sum x0 -> x1, other arithmetic: none -> 2.82 us  [jnp.sum(lax.all_gather(block_here, axis_name='row'), axis=0)]
  transfers between devices with their start and end apart: 5 -> 4, of which waited for: 3 -> 3; matrix products, arithmetic and copies ran while one was open for 42% -> 4% of each run, Pallas kernels for 0% -> 0%
where the time goes in v1:
time: 250 us
  waiting for transfers between devices  112 us (45%)
  matrix products  54.2 us (22%)
  local copies, waits for them, and re-layouts  31.9 us (13%)
  blocking collectives  29.9 us (12%)
  between operations  14.5 us (6%)
  other arithmetic  6.97 us (3%)
    all_gather x1, waiting for transfers between devices, per_device(): full_masked = lax.all_gather(masked, 'ch', axis=1, tiled=True)  49.1 us
    dot_general x1, matrix products, block_grad(): product = jnp.einsum('tij,tif->tjf', tile_set, picked, precision=HIGHEST)  34.5 us
    reduce_scatter x1, waiting for transfers between devices, per_device(): lax.psum_scatter(regrouped, ('row', 'col'), scatter_dimension=0, tiled=True)  31.4 us
    all_gather x1, waiting for transfers between devices, per_device(): grad_rows = lax.all_gather(agg_grad, 'col', axis=0, tiled=True)  31.2 us
    all_to_all x1, blocking collectives, per_device(): lax.all_to_all(partial_value, 'ch', split_axis=1, concat_axis=0, tiled=True)  29.9 us
    dot_general x1, local copies, waits for them, and re-layouts, block_grad(): product = jnp.einsum('tij,tif->tjf', tile_set, picked, precision=HIGHEST)  17.8 us
    gather x1, local copies, waits for them, and re-layouts, block_grad(): picked = jnp.take(blocks, out_tile, axis=0)  11.4 us
    dot_general x1, matrix products, block_grad(): summed = jnp.einsum('tc,tjf->cjf', onehot, product, precision=HIGHEST)  11 us
  transfers between devices with their start and end apart: 4, of which 3 were waited for; matrix products, arithmetic and copies ran while one was open for 4% of the time, Pallas kernels for 0%

profile of v1, /device:TPU:0, one launch (start us, length us, event | category | flops | bytes accessed | tf_op | source)
XLA Modules:
  0.0 249.6 jit_solution(14934166291815169755)
XLA Ops:
  7.2 0.0 all-gather.4.cloned.1.call-start
  7.2 2.1 convert_multiply_fusion
  9.4 0.0 all-gather.4.cloned.1.call-update
  9.4 0.0 all-gather.6.cloned.1.call-start
  9.4 49.1 %all-gather.4.cloned.1.call-done = f32[512,1024]{1,0:T(8,128)} async-done(((f32[512,256]{1,0:T(8,128)}), f32[512,1024]{1,0:T(8,128)}) %all-gather.4.cloned.1.call-update) | async-done | bytes 2097168 | tf_op jit(solution)/shard_map/all_gather | solution.py:32
  58.5 4.2 %fusion.18 = f32[512,256]{1,0:T(8,128)} fusion(f32[512,1024]{1,0:T(8,128)} %all-gather.4.cloned.1.call-done, f32[256,1024]{1,0:T(8,128)S(1)} %copy-done), kind=kOutput, calls=%fused_computation.35 | convolution fusion | flops 1610612736 | bytes 3670016 | tf_op jit(solution)/shard_map/dot_general | solution.py:38
  62.8 0.0 all-gather.6.cloned.1.call-update
  62.8 0.2 all-gather.8.cloned.1.call-start
  63.7 0.7 fusion.14
  64.4 0.7 compare_and_fusion
  65.0 0.7 and_select_fusion.2
  65.7 31.2 %all-gather.6.cloned.1.call-done = f32[2048,256]{1,0:T(8,128)} async-done(((f32[512,256]{1,0:T(8,128)}), f32[2048,256]{1,0:T(8,128)}) %all-gather.6.cloned.1.call-update) | async-done | bytes 2097168 | tf_op jit(solution)/shard_map/all_gather | solution.py:45
  96.9 11.4 %gather_fusion = f32[128,128,256]{2,1,0:T(8,128)} fusion(f32[16,128,256]{2,1,0:T(8,128)} %bitcast.51, s32[1024]{0:T(1024)S(1)} %pad_clamp_fusion), kind=kCustom, calls=%fused_computation | custom fusion | bytes 33554944 | tf_op jit(solution)/shard_map/jit(_take)/gather | solution.py:20
  108.4 34.5 %fusion.2 = f32[128,128,256]{1,2,0:T(8,128)} fusion(f32[128,128,256]{2,1,0:T(8,128)} %gather_fusion, f32[1,1,128,128,128]{4,3,2,1,0:T(8,128)} %param.11, pred[128]{0:T(512)(128)(4,1)S(1)} %compare_and_fusion), kind=kOutput, calls=%fused_computation.3 | convolution fusion | flops 6446645248 | bytes 41943168 | tf_op jit(solution)/shard_map/tij,tif->tjf/dot_general | solution.py:21
  142.9 17.8 %copy.17 = f32[128,128,256]{2,0,1:T(8,128)} copy(f32[128,128,256]{1,2,0:T(8,128)} %fusion.2) | data formatting | bytes 33554432 | tf_op jit(solution)/shard_map/tij,tif->tjf/dot_general | solution.py:21
  160.7 11.0 %fusion.8 = f32[8,128,256]{2,0,1:T(8,128)S(1)} fusion(f32[128,128,256]{2,0,1:T(8,128)} %copy.17, f32[128]{0:T(128)S(1)} %compare_convert_fusion, s32[128]{0:T(128)S(1)} %and_select_fusion.2), kind=kOutput, calls=%fused_computation.9 | convolution fusion | flops 402655232 | bytes 17826816 | tf_op jit(solution)/shard_map/tc,tjf->cjf/dot_general | solution.py:25
  171.6 1.3 copy.18
  173.0 0.0 reduce-scatter.2.cloned.1.call-start
  173.0 4.5 %fusion.17 = f32[1024,256]{1,0:T(8,128)S(1)} fusion(f32[512,1024]{1,0:T(8,128)S(1)} %copy-done.2, f32[512,256]{1,0:T(8,128)} %param.9), kind=kOutput, calls=%fused_computation.34 | convolution fusion | flops 1610612736 | bytes 3670016 | tf_op jit(solution)/shard_map/dot_general | solution.py:33
  177.5 29.9 %all_to_all.19 = f32[256,4,256]{0,2,1:T(8,128)S(1)} all-to-all(f32[256,4,256]{0,2,1:T(8,128)S(1)} %bitcast.52), channel_id=1, replica_groups=mesh['row'=2,'col'=4,'ch'=4] {'ch'}, dimensions={1} | all-to-all | bytes 2097152 | tf_op jit(solution)/shard_map/all_to_all | solution.py:36
  207.5 1.3 copy.15
  208.8 0.0 all-gather.8.cloned.1.call-done
  208.8 2.8 %reduce_sum.9 = f32[1024,256]{1,0:T(8,128)} reduce(f32[2,1024,256]{2,1,0:T(8,128)} %all-gather.8.cloned.1.call-done, f32[]{:T(128)} %constant.39.clone.1), dimensions={0}, to_apply=%region_1.2 | reduce | flops 262144 | bytes 3145732 | tf_op jit(solution)/shard_map/reduce_sum | solution.py:10
  211.7 31.4 %reduce-scatter.2.cloned.1.call-done = f32[128,256]{1,0:T(8,128)} async-done(((f32[1024,256]{1,0:T(8,128)}), f32[128,256]{1,0:T(8,128)}) %reduce-scatter.2.cloned.1.call-update) | async-done | bytes 131088 | tf_op jit(solution)/shard_map/reduce_scatter | solution.py:37
  (10 shorter events, 0.1 us)
Async XLA Ops:
  7.2 51.4 %copy-start = (f32[256,1024]{1,0:T(8,128)S(1)}, f32[256,1024]{1,0:T(8,128)}, u32[]{:S(2)}) copy-start(f32[256,1024]{1,0:T(8,128)} %param.10) | copy-start | bytes 3145732
  7.2 51.4 %all-gather.4.cloned.1.call-start = ((), (), s32[]{:S(2)}) async-start(), calls=%async_computation.2 | async-start | bytes 2621440 | tf_op jit(solution)/shard_map/all_gather | solution.py:32
  9.4 87.5 %all-gather.6.cloned.1.call-start = ((), (), s32[]{:S(2)}) async-start(), calls=%async_computation.4 | async-start | bytes 2621440 | tf_op jit(solution)/shard_map/all_gather | solution.py:45
  62.8 146.0 %all-gather.8.cloned.1.call-start = ((), (), s32[]{:S(2)}) async-start(), calls=%async_computation.5 | async-start | bytes 3145728 | tf_op jit(solution)/shard_map/all_gather | solution.py:10
  142.9 100.2 %copy-start.1 = (f32[256,1024]{1,0:T(8,128)S(1)}, f32[256,1024]{1,0:T(8,128)}, u32[]{:S(2)}) copy-start(f32[256,1024]{1,0:T(8,128)} %param.10) | copy-start | bytes 3145732
  160.7 12.4 %copy-start.2 = (f32[512,1024]{1,0:T(8,128)S(1)}, f32[512,1024]{1,0:T(8,128)}, u32[]{:S(2)}) copy-start(f32[512,1024]{1,0:T(8,128)} %all-gather.4.cloned.1.call-done) | copy-start | bytes 6291460
  173.0 70.1 %reduce-scatter.2.cloned.1.call-start = ((), (), s32[]{:S(2)}) async-start(), calls=%async_computation.3 | async-start | bytes 1179648 | tf_op jit(solution)/shard_map/reduce_scatter | solution.py:37
Sparse Core Ops, SparseCore 0:
  10.1 48.3 all-gather.3
  62.9 33.9 all-gather.5
  173.1 10.5 all-gather.7
  208.9 34.1 reduce-scatter.1
